TPU v7x, 256 devices: a whole 4x4x8 slice. The times are simulated.
256 devices in a mesh: space: 16 (over x_hi, z), tm: 16 (over y, x_lo, core).
Axes of the slice: x: 4 (x_hi: 2, x_lo: 2; x = x_hi * 2 + x_lo), y: 4, z: 8, core: 2. Of those that a mesh axis runs over, the one named last changes fastest.
Arguments:
- snapshots: bfloat16 [163840, 8192], P('space', 'tm'), may hold values from -6 to 6
- modes: bfloat16 [163840, 256], P('space'), may hold values from -0.015625 to 0.015625
Outputs:
- gram: float32 [4864, 4864], P('tm', 'space')
- rhs: float32 [4864, 256], P('tm', 'space')
All inputs are finite; a program needn't handle non-finite values.
Results may differ from a plain program's by a relative error of at most 0.0057.
Values may be sent and summed in bfloat16 or wider, within the bound.
A program may use at most 128 MiB of HBM per device.

v0:
```python
import jax
import jax.numpy as jnp
from jax import lax
from jax.sharding import PartitionSpec as P

LEAD_MODES = 48
ridge_weight = 0.05


def passed_along(value, axis, steps):
    count = lax.axis_size(axis)
    leading, last = (max(0, -steps), min(count, count - steps))
    return lax.ppermute(value, axis, [(source, source + steps) for source in range(leading, last)])


def build_features(current, first, second):
    steps_count = current.shape[1]
    lead = first.shape[0]
    head = current[0:lead].astype(jnp.float32)
    prod_one = (head[:, None, :] * first.astype(jnp.float32)[None, :, :]).reshape(
        lead * lead, steps_count
    )
    prod_two = (head[:, None, :] * second.astype(jnp.float32)[None, :, :]).reshape(
        lead * lead, steps_count
    )
    return jnp.concatenate([current.astype(jnp.float32), prod_one, prod_two], axis=0).astype(
        jnp.bfloat16
    )


def neighbour(values, offset):
    return passed_along(values, "tm", offset)


def contract_rows(left, right):
    return lax.dot_general(
        left, right, (((1,), (1,)), ((), ())), preferred_element_type=jnp.float32
    )


def per_device(snapshots, modes):
    partial_sums = lax.dot_general(
        modes, snapshots, (((0,), (0,)), ((), ())), preferred_element_type=jnp.float32
    )
    coeffs = lax.psum(partial_sums, "space").astype(jnp.bfloat16)
    n_space = lax.axis_size("space")
    n_time = lax.axis_size("tm")
    modes_count = coeffs.shape[0]
    snap_local = coeffs.shape[1]
    total_snaps = snap_local * n_time
    lead = LEAD_MODES
    feature_count = modes_count + 2 * lead * lead
    col_block = feature_count // n_space
    target_block = modes_count // n_space
    row_block = feature_count // n_time
    space_pos = lax.axis_index("space")
    time_pos = lax.axis_index("tm")
    moved = {}
    for offset in (1, 2, -1):
        moved[offset] = neighbour(coeffs, offset)
    phi = build_features(coeffs, moved[1][0:lead], moved[2][0:lead])
    target = moved[-1]
    right = jnp.concatenate(
        [
            lax.dynamic_slice_in_dim(phi, space_pos * col_block, col_block, 0),
            lax.dynamic_slice_in_dim(target, space_pos * target_block, target_block, 0),
        ],
        axis=0,
    )
    joined = lax.psum_scatter(contract_rows(phi, right), "tm", scatter_dimension=0, tiled=True)
    row_global = time_pos * row_block + jnp.arange(row_block, dtype=jnp.int32)
    col_global = space_pos * col_block + jnp.arange(col_block, dtype=jnp.int32)
    diagonal_mask = (row_global[:, None] == col_global[None, :]).astype(jnp.float32)
    gram = joined[:, 0:col_block] / total_snaps + ridge_weight * diagonal_mask
    rhs = joined[:, col_block:] / total_snaps
    return (gram, rhs)


def solution(mesh):
    in_specs = (P("space", "tm"), P("space", None))
    out_specs = (P("tm", "space"), P("tm", "space"))
    return jax.shard_map(
        per_device, mesh=mesh, in_specs=in_specs, out_specs=out_specs, check_vma=False
    )
```

profile of v0, /device:TPU:4, one launch (start us, length us, event | category | flops | bytes accessed | tf_op | source)
XLA Modules:
  0.0 220.1 jit_solution(5401471481429606816)
XLA Ops:
  7.2 0.0 reduce-scatter.2.cloned.1.call-start
  7.2 7.2 %fusion.6 = f32[256,512]{1,0:T(8,128)S(1)} fusion(bf16[10240,256]{1,0:T(8,128)(2,1)} %param.3, bf16[10240,512]{1,0:T(8,128)(2,1)} %param.2), kind=kOutput, calls=%fused_computation.18 | convolution fusion | flops 2684354560 | bytes 16252928 | tf_op jit(solution)/shard_map/dot_general | solution.py:42
  14.4 83.4 %all-reduce.1 = bf16[256,512]{1,0:T(8,128)(2,1)S(1)} all-reduce(f32[256,512]{1,0:T(8,128)S(1)} %fusion.6), channel_id=1, replica_groups=mesh['space'=16,'tm'=16] {'space'}, use_global_device_ids=true, to_apply=%region_0.0 | all-reduce | flops 131072 | bytes 786432 | tf_op jit(solution)/shard_map/psum | solution.py:45
  97.9 4.0 %collective-permute-start.1 = (bf16[256,512]{1,0:T(8,128)(2,1)S(1)}, bf16[256,512]{1,0:T(8,128)(2,1)S(1)}, u32[]{:S(2)}, u32[]{:S(2)}) collective-permute-start(bf16[256,512]{1,0:T(8,128)(2,1)S(1)} %all-reduce.1), channel_id=1, source_target_pairs={{0,2},{1,3},{2,4},{3,5},{4,6},{5,7},{6,8},{7,9},{8,10},{9,11},{10,... | collective-permute-start | bytes 786440 | tf_op jit(solution)/shard_map/ppermute | solution.py:13
  101.9 1.3 collective-permute-start
  103.2 1.3 collective-permute-start.2
  104.6 1.8 collective-permute-done.1
  106.4 0.0 collective-permute-done
  106.4 1.5 multiply_convert_fusion.1
  107.9 0.4 pad_maximum_fusion
  108.3 0.0 collective-permute-done.2
  108.4 9.0 %fusion.1 = f32[4864,320]{1,0:T(8,128)} fusion(bf16[16,512]{1,0:T(8,128)(2,1)S(1)} %constant_dynamic-slice_fusion, bf16[304,512]{1,0:T(8,128)(2,1)S(1)} %constant_dynamic-slice_fusion.1, bf16[2304,512]{1,0:T(8,128)(2,1)S(1)} %bitcast.7, bf16[2304,512]{1,0:T(8,128)(2,1)S(1)} %bitcast.5, bf16[256,512]{1,0:T(8,128)(2,1)S(1)} %all-reduce.1), kind=kOutput, calls=%fused_computation.5 | convolution fusion | flops 1609433088 | bytes 11534336 | tf_op jit(solution)/shard_map/dot_general | solution.py:36
  117.3 0.0 reduce-scatter.2.cloned.1.call-update
  117.4 92.2 %reduce-scatter.2.cloned.1.call-done = f32[304,320]{1,0:T(8,128)} async-done(((f32[4864,320]{1,0:T(8,128)}), f32[304,320]{1,0:T(8,128)}) %reduce-scatter.2.cloned.1.call-update) | async-done | bytes 389136 | tf_op jit(solution)/shard_map/reduce_scatter | solution.py:70
  209.6 1.0 slice_multiply_fusion.1
  210.6 0.7 copy.4
  211.3 1.9 fusion
  (6 shorter events, 0.1 us)
Async XLA Ops:
  7.2 202.4 %reduce-scatter.2.cloned.1.call-start = ((), (), s32[]{:S(2)}) async-start(), calls=%async_computation.1 | async-start | bytes 7938048 | tf_op jit(solution)/shard_map/reduce_scatter | solution.py:70
  97.9 8.5 %collective-permute-start.1 = (bf16[256,512]{1,0:T(8,128)(2,1)S(1)}, bf16[256,512]{1,0:T(8,128)(2,1)S(1)}, u32[]{:S(2)}, u32[]{:S(2)}) collective-permute-start(bf16[256,512]{1,0:T(8,128)(2,1)S(1)} %all-reduce.1), channel_id=1, source_target_pairs={{0,2},{1,3},{2,4},{3,5},{4,6},{5,7},{6,8},{7,9},{8,10},{9,11},{10,... | collective-permute-start | bytes 786440 | tf_op jit(solution)/shard_map/ppermute | solution.py:13
  101.9 4.4 %collective-permute-start = (bf16[256,512]{1,0:T(8,128)(2,1)S(1)}, bf16[256,512]{1,0:T(8,128)(2,1)S(1)}, u32[]{:S(2)}, u32[]{:S(2)}) collective-permute-start(bf16[256,512]{1,0:T(8,128)(2,1)S(1)} %all-reduce.1), channel_id=1, source_target_pairs={{0,1},{1,2},{2,3},{3,4},{4,5},{5,6},{6,7},{7,8},{8,9},{9,10},{10,1... | collective-permute-start | bytes 786440 | tf_op jit(solution)/shard_map/ppermute | solution.py:13
  103.2 5.1 %collective-permute-start.2 = (bf16[256,512]{1,0:T(8,128)(2,1)S(1)}, bf16[256,512]{1,0:T(8,128)(2,1)S(1)}, u32[]{:S(2)}, u32[]{:S(2)}) collective-permute-start(bf16[256,512]{1,0:T(8,128)(2,1)S(1)} %all-reduce.1), channel_id=1, source_target_pairs={{1,0},{2,1},{3,2},{4,3},{5,4},{6,5},{7,6},{8,7},{9,8},{10,9},{11,1... | collective-permute-start | bytes 786440 | tf_op jit(solution)/shard_map/ppermute | solution.py:13
Sparse Core Ops, SparseCore 0:
  117.5 92.0 reduce-scatter.1
where the time goes:
time: 220 us
  waiting for transfers between devices  94 us (43%)
  blocking collectives  83.4 us (38%)
  matrix products  16.2 us (7%)
  between operations  14.2 us (6%)
  starting transfers between devices  6.68 us (3%)
  other arithmetic  4.85 us (2%)
    reduce_scatter x1, waiting for transfers between devices, per_device(): lax.psum_scatter(contract_rows(phi, right), 'tm', scatter_dimension=0, ti...  92.2 us
    psum x1, blocking collectives, per_device(): coeffs = lax.psum(partial_sums, 'space').astype(jnp.bfloat16)  83.4 us
    dot_general x1, matrix products, contract_rows(): lax.dot_general(left, right, (((1,), (1,)), ((), ())), preferred_element_...  8.97 us
    dot_general x1, matrix products, per_device(): lax.dot_general(modes, snapshots, (((0,), (0,)), ((), ())), preferred_ele...  7.22 us
    ppermute x3, starting transfers between devices, passed_along(): lax.ppermute(value, axis, [(source, source + steps) for source in range(l...  6.65 us
  transfers between devices with their start and end apart: 4, of which 2 were waited for; matrix products, arithmetic and copies ran while one was open for 1% of the time, Pallas kernels for 0%

commit v1 on v0

--- a/solution.py
+++ b/solution.py
@@ -42,7 +42,7 @@
     partial_sums = lax.dot_general(
         modes, snapshots, (((0,), (0,)), ((), ())), preferred_element_type=jnp.float32
     )
-    coeffs = lax.psum(partial_sums, "space").astype(jnp.bfloat16)
+    coeffs = jnp.sum(lax.all_gather(partial_sums, "space"), axis=0).astype(jnp.bfloat16)
     n_space = lax.axis_size("space")
     n_time = lax.axis_size("tm")
     modes_count = coeffs.shape[0]

time: 220 us -> 282 us (1.28)
  waiting for transfers between devices: 94 us -> 233 us
  blocking collectives: 83.4 us -> 0 us
  other arithmetic: 4.85 us -> 9.21 us
    all_gather x0 -> x1, waiting for transfers between devices: none -> 136 us  [per_device(): lax.all_gather(partial_sums, 'space')]
    psum x1 -> x0, blocking collectives: 83.4 us -> none  [per_device(): coeffs = lax.psum(partial_sums, 'space').astype(jnp.bfloat16)]
    reduce_sum x0 -> x1, other arithmetic: none -> 4.36 us  [per_device(): jnp.sum(lax.all_gather(partial_sums, 'space'), axis=0).astype(jnp.bfloat16)]
  transfers between devices with their start and end apart: 4 -> 5, of which waited for: 2 -> 3; matrix products, arithmetic and copies ran while one was open for 1% -> 1% of each run, Pallas kernels for 0% -> 0%
where the time goes in v1:
time: 282 us
  waiting for transfers between devices  233 us (83%)
  matrix products  18.3 us (6%)
  between operations  14.2 us (5%)
  other arithmetic  9.21 us (3%)
  starting transfers between devices  6.67 us (2%)
    all_gather x1, waiting for transfers between devices, per_device(): lax.all_gather(partial_sums, 'space')  136 us
    reduce_scatter x1, waiting for transfers between devices, per_device(): lax.psum_scatter(contract_rows(phi, right), 'tm', scatter_dimension=0, ti...  93 us
    dot_general x1, matrix products, per_device(): lax.dot_general(modes, snapshots, (((0,), (0,)), ((), ())), preferred_ele...  9.27 us
    dot_general x1, matrix products, contract_rows(): lax.dot_general(left, right, (((1,), (1,)), ((), ())), preferred_element_...  9 us
    ppermute x3, starting transfers between devices, passed_along(): lax.ppermute(value, axis, [(source, source + steps) for source in range(l...  6.59 us
  transfers between devices with their start and end apart: 5, of which 3 were waited for; matrix products, arithmetic and copies ran while one was open for 1% of the time, Pallas kernels for 0%

profile of v1, /device:TPU:4, one launch (start us, length us, event | category | flops | bytes accessed | tf_op | source)
XLA Modules:
  0.0 281.6 jit_solution(13420012952386546855)
XLA Ops:
  7.2 0.0 all-gather.3.cloned.1.call-start
  7.2 9.3 %fusion.6 = f32[256,512]{1,0:T(8,128)} fusion(bf16[10240,256]{1,0:T(8,128)(2,1)} %param.3, bf16[10240,512]{1,0:T(8,128)(2,1)} %param.2), kind=kOutput, calls=%fused_computation.18 | convolution fusion | flops 2684354560 | bytes 16252928 | tf_op jit(solution)/shard_map/dot_general | solution.py:42
  16.5 0.0 all-gather.3.cloned.1.call-update
  16.5 0.0 reduce-scatter.2.cloned.1.call-start
  16.6 135.8 %all-gather.3.cloned.1.call-done = f32[4096,512]{1,0:T(8,128)} async-done(((f32[256,512]{1,0:T(8,128)}), f32[4096,512]{1,0:T(8,128)}) %all-gather.3.cloned.1.call-update) | async-done | bytes 8388624 | tf_op jit(solution)/shard_map/all_gather | solution.py:45
  152.3 4.4 %reduce_sum.9 = bf16[256,512]{1,0:T(8,128)(2,1)S(1)} reduce(f32[16,256,512]{2,1,0:T(8,128)} %bitcast.9, f32[]{:T(128)} %constant.10.clone.1), dimensions={0}, to_apply=%region_0.0 | reduce | flops 1966080 | bytes 8650756 | tf_op jit(solution)/shard_map/reduce_sum | solution.py:45
  156.7 4.0 %collective-permute-start.1 = (bf16[256,512]{1,0:T(8,128)(2,1)S(1)}, bf16[256,512]{1,0:T(8,128)(2,1)S(1)}, u32[]{:S(2)}, u32[]{:S(2)}) collective-permute-start(bf16[256,512]{1,0:T(8,128)(2,1)S(1)} %reduce_sum.9), channel_id=1, source_target_pairs={{0,2},{1,3},{2,4},{3,5},{4,6},{5,7},{6,8},{7,9},{8,10},{9,11},{10,... | collective-permute-start | bytes 786440 | tf_op jit(solution)/shard_map/ppermute | solution.py:13
  160.7 1.3 collective-permute-start
  162.0 1.3 collective-permute-start.2
  163.3 3.7 %collective-permute-done.1 = bf16[256,512]{1,0:T(8,128)(2,1)S(1)} collective-permute-done((bf16[256,512]{1,0:T(8,128)(2,1)S(1)}, bf16[256,512]{1,0:T(8,128)(2,1)S(1)}, u32[]{:S(2)}, u32[]{:S(2)}) %collective-permute-start.1) | collective-permute-done | bytes 262176 | tf_op jit(solution)/shard_map/ppermute | solution.py:13
  167.0 0.0 collective-permute-done
  167.1 1.5 multiply_convert_fusion.1
  168.6 0.4 pad_maximum_fusion
  169.0 0.0 collective-permute-done.2
  169.0 9.0 %fusion.1 = f32[4864,320]{1,0:T(8,128)} fusion(bf16[16,512]{1,0:T(8,128)(2,1)S(1)} %constant_dynamic-slice_fusion, bf16[304,512]{1,0:T(8,128)(2,1)S(1)} %constant_dynamic-slice_fusion.1, bf16[2304,512]{1,0:T(8,128)(2,1)S(1)} %bitcast.8, bf16[2304,512]{1,0:T(8,128)(2,1)S(1)} %bitcast.6, bf16[256,512]{1,0:T(8,128)(2,1)S(1)} %reduce_sum.9), kind=kOutput, calls=%fused_computation.5 | convolution fusion | flops 1609433088 | bytes 11534336 | tf_op jit(solution)/shard_map/dot_general | solution.py:36
  178.0 0.0 reduce-scatter.2.cloned.1.call-update
  178.1 93.0 %reduce-scatter.2.cloned.1.call-done = f32[304,320]{1,0:T(8,128)} async-done(((f32[4864,320]{1,0:T(8,128)}), f32[304,320]{1,0:T(8,128)}) %reduce-scatter.2.cloned.1.call-update) | async-done | bytes 389136 | tf_op jit(solution)/shard_map/reduce_scatter | solution.py:70
  271.1 1.0 slice_multiply_fusion.1
  272.1 0.7 copy.4
  272.8 1.9 fusion
  (6 shorter events, 0.1 us)
Async XLA Ops:
  7.2 145.1 %all-gather.3.cloned.1.call-start = ((), (), s32[]{:S(2)}) async-start(), calls=%async_computation.2 | async-start | bytes 8912896 | tf_op jit(solution)/shard_map/all_gather | solution.py:45
  16.5 254.6 %reduce-scatter.2.cloned.1.call-start = ((), (), s32[]{:S(2)}) async-start(), calls=%async_computation.1 | async-start | bytes 7938048 | tf_op jit(solution)/shard_map/reduce_scatter | solution.py:70
  156.7 10.3 %collective-permute-start.1 = (bf16[256,512]{1,0:T(8,128)(2,1)S(1)}, bf16[256,512]{1,0:T(8,128)(2,1)S(1)}, u32[]{:S(2)}, u32[]{:S(2)}) collective-permute-start(bf16[256,512]{1,0:T(8,128)(2,1)S(1)} %reduce_sum.9), channel_id=1, source_target_pairs={{0,2},{1,3},{2,4},{3,5},{4,6},{5,7},{6,8},{7,9},{8,10},{9,11},{10,... | collective-permute-start | bytes 786440 | tf_op jit(solution)/shard_map/ppermute | solution.py:13
  160.7 6.4 %collective-permute-start = (bf16[256,512]{1,0:T(8,128)(2,1)S(1)}, bf16[256,512]{1,0:T(8,128)(2,1)S(1)}, u32[]{:S(2)}, u32[]{:S(2)}) collective-permute-start(bf16[256,512]{1,0:T(8,128)(2,1)S(1)} %reduce_sum.9), channel_id=1, source_target_pairs={{0,1},{1,2},{2,3},{3,4},{4,5},{5,6},{6,7},{7,8},{8,9},{9,10},{10,1... | collective-permute-start | bytes 786440 | tf_op jit(solution)/shard_map/ppermute | solution.py:13
  162.0 7.0 %collective-permute-start.2 = (bf16[256,512]{1,0:T(8,128)(2,1)S(1)}, bf16[256,512]{1,0:T(8,128)(2,1)S(1)}, u32[]{:S(2)}, u32[]{:S(2)}) collective-permute-start(bf16[256,512]{1,0:T(8,128)(2,1)S(1)} %reduce_sum.9), channel_id=1, source_target_pairs={{1,0},{2,1},{3,2},{4,3},{5,4},{6,5},{7,6},{8,7},{9,8},{10,9},{11,1... | collective-permute-start | bytes 786440 | tf_op jit(solution)/shard_map/ppermute | solution.py:13
Sparse Core Ops, SparseCore 0:
  16.6 135.6 all-gather.2
  178.2 92.8 reduce-scatter.1
